TPU v7x, 256 devices: a whole 4x4x8 slice. The times are simulated.
256 devices in a mesh: gossip: 16 (over z, x_lo), fsdp: 16 (over x_hi, y, core).
Axes of the slice: x: 4 (x_hi: 2, x_lo: 2; x = x_hi * 2 + x_lo), y: 4, z: 8, core: 2. Of those that a mesh axis runs over, the one named last changes fastest.
Arguments:
- inputs: bfloat16 [16, 2048, 2048], P('gossip', 'fsdp'), may hold values from -6 to 6
- out_grad: bfloat16 [16, 2048, 2048], P('gossip', 'fsdp'), may hold values from -6 to 6
- norm_gain: float32 [16, 2048], P('gossip'), may hold values from 0.5 to 1.5
- w_qkv: bfloat16 [16, 16, 2048, 384], P('gossip', 'fsdp'), may hold values from -64 to 64
- w_out: bfloat16 [16, 16, 128, 2048], P('gossip', 'fsdp'), may hold values from -6 to 6
- mom_qkv: bfloat16 [16, 16, 2048, 384], P('gossip', 'fsdp'), may hold values from -6 to 6
- mom_out: bfloat16 [16, 16, 128, 2048], P('gossip', 'fsdp'), may hold values from -6 to 6
- step_index: int32 [1], replicated, may hold values from 0 to 11
Outputs:
- new_qkv: bfloat16 [16, 16, 2048, 384], P('gossip', 'fsdp')
- new_out: bfloat16 [16, 16, 128, 2048], P('gossip', 'fsdp')
- new_mom_qkv: bfloat16 [16, 16, 2048, 384], P('gossip', 'fsdp')
- new_mom_out: bfloat16 [16, 16, 128, 2048], P('gossip', 'fsdp')
All inputs are finite; a program needn't handle non-finite values.
Results may differ from a plain program's by a relative error of at most 0.0085.
Values may be sent and summed in bfloat16 or wider, within the bound.
A program may use at most 128 MiB of HBM per device.

v0:
```python
from functools import partial
import math
import jax
import jax.numpy as jnp
from jax import lax
from jax.sharding import PartitionSpec as P

HEADS = 16
LEVELS = 3
BETA = 0.9
RATE = 0.1
EPSILON = 1e-05


def for_sending(value):
    return jax.tree.map(lambda a: a.astype(jnp.bfloat16) if a.dtype == jnp.float32 else a, value)


def shifted(value, axis, by):
    size = lax.axis_size(axis)
    return lax.ppermute(value, axis, [(i, (i + by) % size) for i in range(size)])


def rotate(tensor, positions):
    half_width = tensor.shape[-1] // 2
    frequency = jnp.exp(
        -math.log(10000.0) * 2.0 * jnp.arange(half_width, dtype=jnp.float32) / tensor.shape[-1]
    )
    angles = positions.astype(jnp.float32)[:, None] * frequency[None, :]
    cosine = jnp.cos(angles)
    sine_vals = jnp.sin(angles)
    first = tensor[..., :half_width]
    second = tensor[..., half_width:]
    return jnp.concatenate(
        [first * cosine - second * sine_vals, second * cosine + first * sine_vals], -1
    )


def unrotate(grad_in, positions):
    half_width = grad_in.shape[-1] // 2
    frequency = jnp.exp(
        -math.log(10000.0) * 2.0 * jnp.arange(half_width, dtype=jnp.float32) / grad_in.shape[-1]
    )
    angles = positions.astype(jnp.float32)[:, None] * frequency[None, :]
    cosine = jnp.cos(angles)
    sine_vals = jnp.sin(angles)
    first = grad_in[..., :half_width]
    second = grad_in[..., half_width:]
    return jnp.concatenate(
        [first * cosine + second * sine_vals, second * cosine - first * sine_vals], -1
    )


def attend(queries, key_rows, val_rows):
    seq_len, head_dim = queries.shape
    block_len = min(512, seq_len)
    scale = 1.0 / math.sqrt(head_dim)
    outputs = []
    prob_list = []
    for block_num in range(seq_len // block_len):
        begin = block_num * block_len
        key_end = begin + block_len
        scores = (
            jnp.dot(
                queries[begin:key_end], key_rows[:key_end].T, preferred_element_type=jnp.float32
            )
            * scale
        )
        row_pos = begin + jnp.arange(block_len)[:, None]
        col_pos = jnp.arange(key_end)[None, :]
        scores = jnp.where(col_pos <= row_pos, scores, -jnp.inf)
        top = jnp.max(scores, -1, keepdims=True)
        weights = jnp.exp(scores - top)
        weights = weights / jnp.sum(weights, -1, keepdims=True)
        prob_list.append(weights)
        outputs.append(
            jnp.dot(
                weights.astype(jnp.bfloat16), val_rows[:key_end], preferred_element_type=jnp.float32
            )
        )
    return (jnp.concatenate(outputs, 0).astype(jnp.bfloat16), prob_list)


def attend_back(queries, key_rows, val_rows, prob_list, grad_att):
    seq_len, head_dim = queries.shape
    block_len = min(512, seq_len)
    scale = 1.0 / math.sqrt(head_dim)
    grad_q_list = []
    grad_keys = jnp.zeros((seq_len, head_dim), jnp.float32)
    grad_vals = jnp.zeros((seq_len, head_dim), jnp.float32)
    for block_num in range(seq_len // block_len):
        begin = block_num * block_len
        key_end = begin + block_len
        weights = prob_list[block_num]
        weights_b = weights.astype(jnp.bfloat16)
        grad_block = grad_att[begin:key_end]
        grad_probs = jnp.dot(grad_block, val_rows[:key_end].T, preferred_element_type=jnp.float32)
        centred = grad_probs - jnp.sum(weights * grad_probs, -1, keepdims=True)
        grad_scores = (weights * centred * scale).astype(jnp.bfloat16)
        grad_q_list.append(
            jnp.dot(grad_scores, key_rows[:key_end], preferred_element_type=jnp.float32)
        )
        grad_keys = grad_keys.at[:key_end].add(
            jnp.dot(grad_scores.T, queries[begin:key_end], preferred_element_type=jnp.float32)
        )
        grad_vals = grad_vals.at[:key_end].add(
            jnp.dot(weights_b.T, grad_block, preferred_element_type=jnp.float32)
        )
    return (jnp.concatenate(grad_q_list, 0), grad_keys, grad_vals)


def advance(weight, moment, gradient, rate):
    moved_m = (BETA * moment.astype(jnp.float32) + gradient.astype(jnp.float32)).astype(
        jnp.bfloat16
    )
    moved_w = (weight.astype(jnp.float32) - rate * moved_m.astype(jnp.float32)).astype(jnp.bfloat16)
    return (moved_w, moved_m)


def send_updated(payload, by):
    return jax.tree.map(
        lambda part, own: part.astype(own.dtype),
        shifted(for_sending(payload), "gossip", by),
        payload,
    )


def to_partner(mover, payload, step_index):
    branches = [partial(mover, by=1 << bit_level) for bit_level in range(LEVELS)]
    exponent = jnp.remainder(step_index[0], LEVELS)
    return lax.switch(exponent, branches, payload)


def average(own, other):
    return ((own.astype(jnp.float32) + other.astype(jnp.float32)) * 0.5).astype(jnp.bfloat16)


def per_device(inputs, out_grad, norm_gain, w_qkv, w_out, mom_qkv, mom_out, step_index):
    rate = RATE * (step_index[0].astype(jnp.float32) + 1.0) / (4.0 * LEVELS)
    rows_f = inputs[0].astype(jnp.float32)
    stats = lax.rsqrt(jnp.mean(rows_f * rows_f, -1, keepdims=True) + EPSILON)
    normed = (rows_f * stats * norm_gain[0][None, :]).astype(jnp.bfloat16)
    all_normed = lax.all_gather(normed, "fsdp", axis=0, tiled=True)
    seq_len, width = all_normed.shape
    head_qkv = w_qkv[0]
    head_out = w_out[0]
    head_count, head_dim = (head_out.shape[0], head_out.shape[1])
    positions = jnp.arange(seq_len)
    out_scale = 1.0 / math.sqrt(HEADS * head_dim)
    projected = jnp.einsum(
        "td,hde->hte", all_normed, head_qkv, preferred_element_type=jnp.float32
    ) * (1.0 / math.sqrt(width))
    queries = rotate(projected[..., :head_dim], positions).astype(jnp.bfloat16)
    key_rows = rotate(projected[..., head_dim : 2 * head_dim], positions).astype(jnp.bfloat16)
    val_rows = projected[..., 2 * head_dim :].astype(jnp.bfloat16)
    attended, prob_list = jax.vmap(attend)(queries, key_rows, val_rows)
    piece = lax.all_gather(out_grad[0], "fsdp", axis=0, tiled=True)
    out_sum = jnp.zeros((head_count, head_dim, width), jnp.float32)
    count = piece.shape[0]
    att_rows = lax.slice_in_dim(attended, 0, count, axis=1)
    out_sum = out_sum + jnp.einsum(
        "hte,td->hed", att_rows, piece, preferred_element_type=jnp.float32
    )
    new_rows = (
        jnp.einsum("td,hed->hte", piece, head_out, preferred_element_type=jnp.float32) * out_scale
    ).astype(jnp.bfloat16)
    grad_att = new_rows
    out_sum, grad_att = (out_sum, grad_att)
    grad_out = (out_sum * out_scale).astype(jnp.bfloat16)
    grad_q, grad_k, grad_v = jax.vmap(attend_back)(queries, key_rows, val_rows, prob_list, grad_att)
    grad_proj = jnp.concatenate(
        [unrotate(grad_q, positions), unrotate(grad_k, positions), grad_v], -1
    )
    grad_proj = (grad_proj * (1.0 / math.sqrt(width))).astype(jnp.bfloat16)
    grad_qkv = jnp.einsum(
        "td,hte->hde", all_normed, grad_proj, preferred_element_type=jnp.float32
    ).astype(jnp.bfloat16)[None]
    grad_out = grad_out[None]
    moved_qkv, moved_mqkv = advance(w_qkv, mom_qkv, grad_qkv, rate)
    moved_out, moved_mout = advance(w_out, mom_out, grad_out, rate)
    other_qkv, other_out, other_mqkv, other_mout = to_partner(
        send_updated, (moved_qkv, moved_out, moved_mqkv, moved_mout), step_index
    )
    return (
        average(moved_qkv, other_qkv),
        average(moved_out, other_out),
        average(moved_mqkv, other_mqkv),
        average(moved_mout, other_mout),
    )


def solution(mesh):
    return jax.shard_map(
        per_device,
        mesh=mesh,
        in_specs=(
            P("gossip", "fsdp", None),
            P("gossip", "fsdp", None),
            P("gossip", None),
            P("gossip", "fsdp", None, None),
            P("gossip", "fsdp", None, None),
            P("gossip", "fsdp", None, None),
            P("gossip", "fsdp", None, None),
            P(),
        ),
        out_specs=(
            P("gossip", "fsdp", None, None),
            P("gossip", "fsdp", None, None),
            P("gossip", "fsdp", None, None),
            P("gossip", "fsdp", None, None),
        ),
        check_vma=False,
    )
```

profile of v0, /device:TPU:1, one launch (start us, length us, event | category | flops | bytes accessed | tf_op | source)
XLA Modules:
  0.0 339.4 jit_solution(3943303239801922108)
XLA Ops:
  7.2 1.4 fusion.63
  8.6 2.0 fusion.65
  12.1 1.6 copy.12
  13.7 1.6 copy.13
  15.4 77.8 %all-gather.4.cloned.1.call-done = bf16[2048,2048]{1,0:T(8,128)(2,1)} async-done(((bf16[128,2048]{1,0:T(8,128)(2,1)}), bf16[2048,2048]{1,0:T(8,128)(2,1)}) %all-gather.4.cloned.1.call-update) | async-done | bytes 8388624 | tf_op jit(solution)/shard_map/all_gather | solution.py:143
  93.2 5.9 %fusion.158 = (bf16[1,2048,384]{1,2,0:T(8,128)(2,1)S(1)}, f32[1,2048,384]{1,2,0:T(8,128)S(1)}) fusion(bf16[2048,2048]{1,0:T(8,128)(2,1)} %all-gather.4.cloned.1.call-done, bf16[1,1,2048,384]{3,2,1,0:T(8,128)(2,1)S(1)} %copy-done.5), kind=kOutput, calls=%fused_computation.199 | convolution fusion | flops 3222798336 | bytes 14680064 | tf_op jit(solution)/shard_map/td,hde->hte/dot_general | solution.py:150
  99.1 2.6 fusion.93
  102.7 68.8 %all-gather.6.cloned.1.call-done = bf16[1,2048,2048]{2,1,0:T(8,128)(2,1)} async-done(((bf16[1,128,2048]{2,1,0:T(8,128)(2,1)}), bf16[1,2048,2048]{2,1,0:T(8,128)(2,1)}) %all-gather.6.cloned.1.call-update) | async-done | bytes 8388624 | tf_op jit(solution)/shard_map/all_gather | solution.py:157
  171.6 6.3 %fusion.35 = bf16[1,2048,128]{1,2,0:T(8,128)(2,1)S(1)} fusion(bf16[1,2048,2048]{2,1,0:T(8,128)(2,1)} %all-gather.6.cloned.1.call-done, bf16[1,1,128,2048]{3,2,1,0:T(8,128)(2,1)S(1)} %copy-done.1), kind=kOutput, calls=%fused_computation.48 | convolution fusion | flops 1074266112 | bytes 9437184 | tf_op jit(solution)/shard_map/td,hed->hte/dot_general | solution.py:165
  178.2 1.1 copy-done.10
  182.0 0.8 fusion.160
  183.4 0.7 convolution_convert_fusion.4
  184.1 1.0 multiply_reduce_fusion.1
  185.1 1.0 fusion.159
  186.1 0.7 fusion.5
  186.8 0.9 convolution_convert_fusion.1
  187.7 1.2 multiply_reduce_fusion
  190.9 0.9 fusion.18
  193.4 0.9 multiply_convert_fusion.3
  195.4 1.5 multiply_convert_fusion
  196.9 0.9 convolution_bitcast_fusion.9
  198.3 2.1 fusion.98
  200.4 2.1 fusion.101
  202.5 2.1 fusion.104
  204.6 2.2 fusion.107
  206.8 1.0 fusion.22
  208.7 1.3 slice-done.3
  210.0 3.8 %fusion.8 = (bf16[1,1,2048,384]{2,3,1,0:T(8,128)(2,1)S(1)}, bf16[1,1,2048,384]{2,3,1,0:T(8,128)(2,1)S(1)}) fusion(bf16[1,1,2048,384]{2,3,1,0:T(8,128)(2,1)S(1)} %copy-done.6, f32[]{:T(128)} %bitcast, bf16[2048,2048]{1,0:T(8,128)(2,1)S(1)} %bitcast.244, f32[2048,384]{0,1:T(8,128)S(1)} %fusion.22, bf16[1,1,2048,384]{2,3,1,0:T(8,128)(2,1)S(1)} %copy-done.7), kind=kOutput, calls=%fused_computation.16 | convolution fusion | flops 3231449088 | bytes 17825796 | tf_op jit(solution)/shard_map/td,hte->hde/dot_general | solution.py:175
  213.8 2.4 fusion.60
  216.2 102.7 %conditional.3 = (f32[1,1,128,2048]{3,2,1,0:T(8,128)}, f32[1,1,128,2048]{3,2,1,0:T(8,128)}, f32[1,1,2048,384]{2,3,1,0:T(8,128)}, f32[1,1,2048,384]{2,3,1,0:T(8,128)}) conditional(s32[]{:T(128)} %clamp.3, (bf16[1,1,2048,384]{2,3,1,0:T(8,128)(2,1)S(1)}, bf16[1,1,128,2048]{3,2,1,0:T(8,128)(2,1)}, ...), branch_computations={%region_13.14_spmd, %region_14.15_spmd, %region_15.16_spmd} | conditional | flops 524288 | bytes 35651776
  216.2 1.6 copy.20
  217.8 1.3 collective-permute-start.4
  219.1 1.6 copy.21
  220.6 1.3 collective-permute-start.6
  221.9 1.3 collective-permute-start.5
  223.2 2.5 collective-permute-start.7
  225.7 74.8 %collective-permute-done.5 = bf16[1,1,128,2048]{3,2,1,0:T(8,128)(2,1)S(1)} collective-permute-done((bf16[1,1,128,2048]{3,2,1,0:T(8,128)(2,1)}, bf16[1,1,128,2048]{3,2,1,0:T(8,128)(2,1)S(1)}, u32[]{:S(2)}, u32[]{:S(2)}) %collective-permute-start.5) | collective-permute-done | bytes 524320 | tf_op jit(solution)/shard_map/cond/branch_1_fun/ppermute | solution.py:21
  300.5 1.2 convert_element_type.309
  301.6 10.1 %collective-permute-done.7 = bf16[1,1,128,2048]{3,2,1,0:T(8,128)(2,1)S(1)} collective-permute-done((bf16[1,1,128,2048]{3,2,1,0:T(8,128)(2,1)}, bf16[1,1,128,2048]{3,2,1,0:T(8,128)(2,1)S(1)}, u32[]{:S(2)}, u32[]{:S(2)}) %collective-permute-start.7) | collective-permute-done | bytes 524320 | tf_op jit(solution)/shard_map/cond/branch_1_fun/ppermute | solution.py:21
  311.7 1.1 convert_element_type.315
  312.8 3.1 copy.33
  315.9 3.1 copy.36
  318.9 2.3 fusion.62
  321.2 3.5 %fusion.10 = bf16[1,1,2048,384]{2,3,1,0:T(8,128)(2,1)} fusion(f32[1,1,2048,384]{2,3,1,0:T(8,128)} %get-tuple-element.205, bf16[1,1,2048,384]{2,3,1,0:T(8,128)(2,1)S(1)} %get-tuple-element.229), kind=kLoop, calls=%fused_computation.18 | loop fusion | flops 3145728 | bytes 6291456 | tf_op jit(solution)/shard_map/convert_element_type | solution.py:135
  324.7 2.7 copy.27
  327.4 0.9 multiply_convert_fusion.6
  328.4 2.4 multiply_convert_fusion.1
  330.8 1.6 copy.26
  (66 shorter events, 11.4 us)
Async XLA Ops:
  7.2 4.9 %copy-start.5 = (bf16[1,1,2048,384]{3,2,1,0:T(8,128)(2,1)S(1)}, bf16[1,1,2048,384]{3,2,1,0:T(8,128)(2,1)}, u32[]{:S(2)}) copy-start(bf16[1,1,2048,384]{3,2,1,0:T(8,128)(2,1)} %param.34) | copy-start | bytes 4718596
  7.2 6.6 %copy-start.4 = (bf16[1,1,2048,384]{3,2,1,0:T(8,128)(2,1)S(1)}, bf16[1,1,2048,384]{3,2,1,0:T(8,128)(2,1)}, u32[]{:S(2)}) copy-start(bf16[1,1,2048,384]{3,2,1,0:T(8,128)(2,1)} %param.36) | copy-start | bytes 4718596
  7.2 86.1 %all-gather.4.cloned.1.call-start = ((), (), s32[]{:S(2)}) async-start(), calls=%async_computation | async-start | bytes 8912896 | tf_op jit(solution)/shard_map/all_gather | solution.py:143
  10.7 160.9 %all-gather.6.cloned.1.call-start = ((), (), s32[]{:S(2)}) async-start(), calls=%async_computation.1 | async-start | bytes 8912896 | tf_op jit(solution)/shard_map/all_gather | solution.py:157
  99.1 3.2 copy-start.9
  102.1 69.4 %copy-start.1 = (bf16[1,1,128,2048]{3,2,1,0:T(8,128)(2,1)S(1)}, bf16[1,1,128,2048]{3,2,1,0:T(8,128)(2,1)}, u32[]{:S(2)}) copy-start(bf16[1,1,128,2048]{3,2,1,0:T(8,128)(2,1)} %param.35) | copy-start | bytes 1572868
  177.9 1.4 copy-start.10
  198.3 9.6 %slice-start.2 = ((s8[8388608]{0:T(1024)(128)(4,1)}), s8[4194304]{0:T(1024)(128)(4,1)S(1)}, s32[]{:S(2)}) async-start(s8[8388608]{0:T(1024)(128)(4,1)} %bitcast.243), calls=%async_computation.4 | async-start | bytes 8388608
  206.8 1.4 copy-start.6
  206.8 1.9 copy-start.7
  206.8 3.1 slice-start.3
  206.8 6.9 %slice-start = ((s8[8388608]{0:T(1024)(128)(4,1)}), s8[4194304]{0:T(1024)(128)(4,1)S(1)}, s32[]{:S(2)}) async-start(s8[8388608]{0:T(1024)(128)(4,1)} %bitcast.236), calls=%async_computation.2 | async-start | bytes 8388608
  210.0 3.8 %slice-start.1 = ((s8[8388608]{0:T(1024)(128)(4,1)}), s8[4194304]{0:T(1024)(128)(4,1)S(1)}, s32[]{:S(2)}) async-start(s8[8388608]{0:T(1024)(128)(4,1)} %bitcast.236), calls=%async_computation.3 | async-start | bytes 8388608
  210.0 3.8 %copy-start.2 = (bf16[1,1,128,2048]{3,2,1,0:T(8,128)(2,1)S(1)}, bf16[1,1,128,2048]{3,2,1,0:T(8,128)(2,1)}, u32[]{:S(2)}) copy-start(bf16[1,1,128,2048]{3,2,1,0:T(8,128)(2,1)} %param.35) | copy-start | bytes 1572868
  210.0 3.8 %copy-start.8 = (bf16[1,1,128,2048]{3,2,1,0:T(8,128)(2,1)S(1)}, bf16[1,1,128,2048]{3,2,1,0:T(8,128)(2,1)}, u32[]{:S(2)}) copy-start(bf16[1,1,128,2048]{3,2,1,0:T(8,128)(2,1)} %param.37) | copy-start | bytes 1572868
  217.8 95.0 %collective-permute-start.4 = (bf16[1,1,2048,384]{3,2,1,0:T(8,128)(2,1)}, bf16[1,1,2048,384]{3,2,1,0:T(8,128)(2,1)}, u32[]{:S(2)}, u32[]{:S(2)}) collective-permute-start(bf16[1,1,2048,384]{3,2,1,0:T(8,128)(2,1)} %copy.20), channel_id=1, source_target_pairs={{0,32},{16,48},{32,64},{48,80},{64,96},{80,112},{96,128},{112,144}... | collective-permute-start | bytes 4718600 | tf_op jit(solution)/shard_map/cond/branch_1_fun/ppermute | solution.py:21
  220.6 95.2 %collective-permute-start.6 = (bf16[1,1,2048,384]{3,2,1,0:T(8,128)(2,1)}, bf16[1,1,2048,384]{3,2,1,0:T(8,128)(2,1)}, u32[]{:S(2)}, u32[]{:S(2)}) collective-permute-start(bf16[1,1,2048,384]{3,2,1,0:T(8,128)(2,1)} %copy.21), channel_id=1, source_target_pairs={{0,32},{16,48},{32,64},{48,80},{64,96},{80,112},{96,128},{112,144}... | collective-permute-start | bytes 4718600 | tf_op jit(solution)/shard_map/cond/branch_1_fun/ppermute | solution.py:21
  221.9 78.6 %collective-permute-start.5 = (bf16[1,1,128,2048]{3,2,1,0:T(8,128)(2,1)}, bf16[1,1,128,2048]{3,2,1,0:T(8,128)(2,1)S(1)}, u32[]{:S(2)}, u32[]{:S(2)}) collective-permute-start(bf16[1,1,128,2048]{3,2,1,0:T(8,128)(2,1)} %get-tuple-element.165), channel_id=1, source_target_pairs={{0,32},{16,48},{32,64},{48,80},{64,96},{80,112},{96,128},{112,144}... | collective-permute-start | bytes 1572872 | tf_op jit(solution)/shard_map/cond/branch_1_fun/ppermute | solution.py:21
  223.2 88.5 %collective-permute-start.7 = (bf16[1,1,128,2048]{3,2,1,0:T(8,128)(2,1)}, bf16[1,1,128,2048]{3,2,1,0:T(8,128)(2,1)S(1)}, u32[]{:S(2)}, u32[]{:S(2)}) collective-permute-start(bf16[1,1,128,2048]{3,2,1,0:T(8,128)(2,1)} %get-tuple-element.167), channel_id=1, source_target_pairs={{0,32},{16,48},{32,64},{48,80},{64,96},{80,112},{96,128},{112,144}... | collective-permute-start | bytes 1572872 | tf_op jit(solution)/shard_map/cond/branch_1_fun/ppermute | solution.py:21
  324.7 2.7 copy-start
  324.7 2.7 copy-start.3
Sparse Core Ops, SparseCore 0:
  11.3 81.8 all-gather.3
  96.0 75.5 all-gather.5
where the time goes:
time: 343 us; the launch traced here: 339 us
  waiting for transfers between devices  232 us (68%)
  matrix products  33.6 us (10%)
  other arithmetic  31.2 us (9%)
  local copies, waits for them, and re-layouts  20.5 us (6%)
  between operations  15.3 us (4%)
  starting transfers between devices  6.38 us (2%)
    ppermute x4, waiting for transfers between devices, shifted(): lax.ppermute(value, axis, [(i, (i + by) % size) for i in range(size)])  84.9 us
    all_gather x1, waiting for transfers between devices, per_device(): all_normed = lax.all_gather(normed, 'fsdp', axis=0, tiled=True)  77.8 us
    all_gather x1, waiting for transfers between devices, per_device(): piece = lax.all_gather(out_grad[0], 'fsdp', axis=0, tiled=True)  68.8 us
    unnamed x34, local copies, waits for them, and re-layouts  10.7 us
    another operation x4, local copies, waits for them, and re-layouts  9.23 us
    convert_element_type x4, other arithmetic, average(): ((own.astype(jnp.float32) + other.astype(jnp.float32)) * 0.5).astype(jnp....  9.15 us
    unnamed x6, other arithmetic  8.45 us
  transfers between devices with their start and end apart: 6, of which 4 were waited for; matrix products, arithmetic and copies ran while one was open for 6% of the time, Pallas kernels for 0%

commit v1 on v0

--- a/solution.py
+++ b/solution.py
@@ -154,7 +154,15 @@
     key_rows = rotate(projected[..., head_dim : 2 * head_dim], positions).astype(jnp.bfloat16)
     val_rows = projected[..., 2 * head_dim :].astype(jnp.bfloat16)
     attended, prob_list = jax.vmap(attend)(queries, key_rows, val_rows)
-    piece = lax.all_gather(out_grad[0], "fsdp", axis=0, tiled=True)
+    piece = jnp.concatenate(
+        lax.all_to_all(
+            jnp.stack(lax.axis_size("fsdp") * [out_grad[0]]),
+            axis_name="fsdp",
+            split_axis=0,
+            concat_axis=0,
+        ),
+        axis=0,
+    )
     out_sum = jnp.zeros((head_count, head_dim, width), jnp.float32)
     count = piece.shape[0]
     att_rows = lax.slice_in_dim(attended, 0, count, axis=1)

time: 343 us -> 359 us (1.047)
  starting transfers between devices: 6.38 us -> 15.5 us
  matrix products: 33.6 us -> 37.5 us
    all_to_all x0 -> x1, waiting for transfers between devices: none -> 126 us  [per_device(): lax.all_to_all(jnp.stack(lax.axis_size('fsdp') * [out_grad[0]]), axis_nam...]
    all_gather x1 -> x0, waiting for transfers between devices: 68.8 us -> none  [per_device(): piece = lax.all_gather(out_grad[0], 'fsdp', axis=0, tiled=True)]
    all_gather x1, waiting for transfers between devices: 77.8 us -> 17.5 us  [per_device(): all_normed = lax.all_gather(normed, 'fsdp', axis=0, tiled=True)]
    all_to_all x0 -> x1, starting transfers between devices: none -> 8.44 us  [per_device(): lax.all_to_all(jnp.stack(lax.axis_size('fsdp') * [out_grad[0]]), axis_nam...]
    another operation x4 -> x5, local copies, waits for them, and re-layouts: 9.23 us -> 14.6 us
    dot_general x1, matrix products: 2.42 us -> 6.12 us  [per_device(): jnp.einsum('hte,td->hed', att_rows, piece, preferred_element_type=jnp.flo...]
    unnamed x34 -> x24, local copies, waits for them, and re-layouts: 10.7 us -> 8.57 us
    unnamed x6 -> x5, other arithmetic: 8.45 us -> 8.45 us
where the time goes in v1:
time: 359 us; the launch traced here: 353 us
  waiting for transfers between devices  230 us (64%)
  matrix products  37.5 us (10%)
  other arithmetic  31.2 us (9%)
  local copies, waits for them, and re-layouts  23.4 us (7%)
  between operations  15.8 us (4%)
  starting transfers between devices  15.5 us (4%)
    all_to_all x1, waiting for transfers between devices, per_device(): lax.all_to_all(jnp.stack(lax.axis_size('fsdp') * [out_grad[0]]), axis_nam...  126 us
    ppermute x4, waiting for transfers between devices, shifted(): lax.ppermute(value, axis, [(i, (i + by) % size) for i in range(size)])  85.5 us
    all_gather x1, waiting for transfers between devices, per_device(): all_normed = lax.all_gather(normed, 'fsdp', axis=0, tiled=True)  17.5 us
    another operation x4, local copies, waits for them, and re-layouts  9.27 us
    convert_element_type x4, other arithmetic, average(): ((own.astype(jnp.float32) + other.astype(jnp.float32)) * 0.5).astype(jnp....  9.15 us
    unnamed x24, local copies, waits for them, and re-layouts  8.57 us
    unnamed x5, other arithmetic  8.45 us
    all_to_all x1, starting transfers between devices, per_device(): lax.all_to_all(jnp.stack(lax.axis_size('fsdp') * [out_grad[0]]), axis_nam...  8.44 us
  transfers between devices with their start and end apart: 6, of which 4 were waited for; matrix products, arithmetic and copies ran while one was open for 6% of the time, Pallas kernels for 0%

profile of v1, /device:TPU:1, one launch (start us, length us, event | category | flops | bytes accessed | tf_op | source)
XLA Modules:
  0.0 352.8 jit_solution(5419188947566011367)
XLA Ops:
  7.2 1.2 fusion.39
  8.4 2.0 fusion.41
  10.5 5.3 %stack.3 = bf16[16,128,2048]{2,1,0:T(8,128)(2,1)} broadcast(bf16[128,2048]{1,0:T(8,128)(2,1)} %bitcast.219), dimensions={1,2} | broadcast | bytes 8912896 | tf_op jit(solution)/shard_map/stack | solution.py:159
  15.8 8.4 %all-to-all-start = ((bf16[16,128,2048]{2,1,0:T(8,128)(2,1)}), bf16[16,128,2048]{2,1,0:T(8,128)(2,1)}, u32[]{:S(2)}, u32[]{:S(2)}) async-start(bf16[16,128,2048]{2,1,0:T(8,128)(2,1)} %stack.3), calls=%async_computation | async-start | bytes 16777216 | tf_op jit(solution)/shard_map/all_to_all | solution.py:158
  25.1 2.6 copy.12
  27.7 1.6 copy.13
  29.4 126.5 %all-to-all-done = bf16[16,128,2048]{2,1,0:T(8,128)(2,1)} async-done(((bf16[16,128,2048]{2,1,0:T(8,128)(2,1)}), bf16[16,128,2048]{2,1,0:T(8,128)(2,1)}, u32[]{:S(2)}, u32[]{:S(2)}) %all-to-all-start) | async-done | bytes 8388640 | tf_op jit(solution)/shard_map/all_to_all | solution.py:158
  155.9 6.4 %fusion.25 = bf16[1,2048,128]{1,2,0:T(8,128)(2,1)S(1)} fusion(bf16[2048,2048]{1,0:T(8,128)(2,1)} %bitcast.14, bf16[1,1,128,2048]{3,2,1,0:T(8,128)(2,1)S(1)} %copy-done.1), kind=kOutput, calls=%fused_computation.48 | convolution fusion | flops 1074266112 | bytes 9437184 | tf_op jit(solution)/shard_map/td,hed->hte/dot_general | solution.py:173
  162.3 17.5 %all-gather.2.cloned.1.call-done = bf16[2048,2048]{1,0:T(8,128)(2,1)} async-done(((bf16[128,2048]{1,0:T(8,128)(2,1)}), bf16[2048,2048]{1,0:T(8,128)(2,1)}) %all-gather.2.cloned.1.call-update) | async-done | bytes 8388624 | tf_op jit(solution)/shard_map/all_gather | solution.py:143
  179.8 5.9 %fusion.134 = (bf16[1,2048,384]{1,2,0:T(8,128)(2,1)S(1)}, f32[1,2048,384]{1,2,0:T(8,128)S(1)}) fusion(bf16[2048,2048]{1,0:T(8,128)(2,1)} %all-gather.2.cloned.1.call-done, bf16[1,1,2048,384]{3,2,1,0:T(8,128)(2,1)S(1)} %copy-done.4), kind=kOutput, calls=%fused_computation.195 | convolution fusion | flops 3222798336 | bytes 14680064 | tf_op jit(solution)/shard_map/td,hde->hte/dot_general | solution.py:150
  185.7 2.6 fusion.69
  192.4 0.8 fusion.136
  193.8 0.7 convolution_convert_fusion.4
  194.5 1.0 multiply_reduce_fusion.1
  195.5 1.0 fusion.135
  196.5 0.7 fusion.1
  197.2 0.9 convolution_convert_fusion.1
  198.1 1.2 multiply_reduce_fusion
  200.9 0.9 fusion.14
  203.8 0.9 multiply_convert_fusion.3
  205.8 1.5 multiply_convert_fusion
  207.3 0.8 convolution_bitcast_fusion.9
  208.7 2.1 fusion.74
  210.8 2.1 fusion.77
  212.9 2.1 fusion.80
  214.9 2.2 fusion.83
  217.2 1.1 fusion.18
  218.3 6.1 %fusion.36 = (bf16[1,1,128,2048]{3,2,1,0:T(8,128)(2,1)}, bf16[1,1,128,2048]{3,2,1,0:T(8,128)(2,1)}) fusion(bf16[1,1,128,2048]{3,2,1,0:T(8,128)(2,1)S(1)} %copy-done.1, f32[]{:T(128)} %bitcast, bf16[2048,2048]{1,0:T(8,128)(2,1)} %bitcast.14, bf16[512,128]{1,0:T(8,128)(2,1)S(1)} %convolution_convert_fusion.1, ...), kind=kOutput, calls=%fused_computation.81 | convolution fusion | flops 1078984704 | bytes 11010052 | tf_op jit(solution)/shard_map/hte,td->hed/dot_general | solution.py:169
  224.4 3.9 %fusion.4 = (bf16[1,1,2048,384]{2,3,1,0:T(8,128)(2,1)S(1)}, bf16[1,1,2048,384]{2,3,1,0:T(8,128)(2,1)S(1)}) fusion(bf16[1,1,2048,384]{2,3,1,0:T(8,128)(2,1)S(1)} %copy-done.5, f32[]{:T(128)} %bitcast, bf16[2048,2048]{1,0:T(8,128)(2,1)S(1)} %bitcast.222, f32[2048,384]{0,1:T(8,128)S(1)} %fusion.18, bf16[1,1,2048,384]{2,3,1,0:T(8,128)(2,1)S(1)} %copy-done.6), kind=kOutput, calls=%fused_computation.12 | convolution fusion | flops 3231449088 | bytes 17825796 | tf_op jit(solution)/shard_map/td,hte->hde/dot_general | solution.py:183
  228.3 104.1 %conditional.3 = (f32[1,1,128,2048]{3,2,1,0:T(8,128)}, f32[1,1,128,2048]{3,2,1,0:T(8,128)}, f32[1,1,2048,384]{2,3,1,0:T(8,128)}, f32[1,1,2048,384]{2,3,1,0:T(8,128)}) conditional(s32[]{:T(128)} %clamp.3, (bf16[1,1,2048,384]{2,3,1,0:T(8,128)(2,1)S(1)}, bf16[1,1,128,2048]{3,2,1,0:T(8,128)(2,1)}, ...), branch_computations={%region_13.14_spmd, %region_14.15_spmd, %region_15.16_spmd} | conditional | flops 524288 | bytes 35651776
  228.3 1.6 copy.20
  229.9 1.5 collective-permute-start.4
  231.4 1.6 copy.21
  232.9 1.5 collective-permute-start.6
  234.4 1.4 collective-permute-start.5
  235.8 2.6 collective-permute-start.7
  238.5 75.4 %collective-permute-done.5 = bf16[1,1,128,2048]{3,2,1,0:T(8,128)(2,1)S(1)} collective-permute-done((bf16[1,1,128,2048]{3,2,1,0:T(8,128)(2,1)}, bf16[1,1,128,2048]{3,2,1,0:T(8,128)(2,1)S(1)}, u32[]{:S(2)}, u32[]{:S(2)}) %collective-permute-start.5) | collective-permute-done | bytes 524320 | tf_op jit(solution)/shard_map/cond/branch_1_fun/ppermute | solution.py:21
  313.9 1.2 convert_element_type.309
  315.1 10.1 %collective-permute-done.7 = bf16[1,1,128,2048]{3,2,1,0:T(8,128)(2,1)S(1)} collective-permute-done((bf16[1,1,128,2048]{3,2,1,0:T(8,128)(2,1)}, bf16[1,1,128,2048]{3,2,1,0:T(8,128)(2,1)S(1)}, u32[]{:S(2)}, u32[]{:S(2)}) %collective-permute-start.7) | collective-permute-done | bytes 524320 | tf_op jit(solution)/shard_map/cond/branch_1_fun/ppermute | solution.py:21
  325.1 1.1 convert_element_type.315
  326.2 3.1 copy.33
  329.3 3.1 copy.36
  332.4 2.3 fusion.38
  334.7 3.5 fusion.6
  338.2 2.7 copy.27
  340.9 0.9 multiply_convert_fusion.6
  341.8 2.4 multiply_convert_fusion.1
  344.2 1.6 copy.26
  (55 shorter events, 9.5 us)
Async XLA Ops:
  7.2 172.6 %all-gather.2.cloned.1.call-start = ((), (), s32[]{:S(2)}) async-start(), calls=%async_computation.1 | async-start | bytes 8912896 | tf_op jit(solution)/shard_map/all_gather | solution.py:143
  15.8 140.0 %all-to-all-start = ((bf16[16,128,2048]{2,1,0:T(8,128)(2,1)}), bf16[16,128,2048]{2,1,0:T(8,128)(2,1)}, u32[]{:S(2)}, u32[]{:S(2)}) async-start(bf16[16,128,2048]{2,1,0:T(8,128)(2,1)} %stack.3), calls=%async_computation | async-start | bytes 16777216 | tf_op jit(solution)/shard_map/all_to_all | solution.py:158
  24.3 3.4 copy-start.3
  25.1 130.8 %copy-start.1 = (bf16[1,1,128,2048]{3,2,1,0:T(8,128)(2,1)S(1)}, bf16[1,1,128,2048]{3,2,1,0:T(8,128)(2,1)}, u32[]{:S(2)}) copy-start(bf16[1,1,128,2048]{3,2,1,0:T(8,128)(2,1)} %param.35) | copy-start | bytes 1572868
  155.9 23.9 %copy-start.4 = (bf16[1,1,2048,384]{3,2,1,0:T(8,128)(2,1)S(1)}, bf16[1,1,2048,384]{3,2,1,0:T(8,128)(2,1)}, u32[]{:S(2)}) copy-start(bf16[1,1,2048,384]{3,2,1,0:T(8,128)(2,1)} %param.34) | copy-start | bytes 4718596
  212.8 11.6 %slice-start = ((s8[8388608]{0:T(1024)(128)(4,1)}), s8[4194304]{0:T(1024)(128)(4,1)S(1)}, s32[]{:S(2)}) async-start(s8[8388608]{0:T(1024)(128)(4,1)} %bitcast.221), calls=%async_computation.2 | async-start | bytes 8388608
  217.2 1.1 copy-start.7
  217.2 7.2 %slice-start.1 = ((s8[8388608]{0:T(1024)(128)(4,1)}), s8[4194304]{0:T(1024)(128)(4,1)S(1)}, s32[]{:S(2)}) async-start(s8[8388608]{0:T(1024)(128)(4,1)} %bitcast.221), calls=%async_computation.3 | async-start | bytes 8388608
  218.3 6.1 %copy-start.5 = (bf16[1,1,2048,384]{2,3,1,0:T(8,128)(2,1)S(1)}, bf16[1,1,2048,384]{2,3,1,0:T(8,128)(2,1)}, u32[]{:S(2)}) copy-start(bf16[1,1,2048,384]{2,3,1,0:T(8,128)(2,1)} %copy.12) | copy-start | bytes 4718596
  218.3 6.1 %copy-start.6 = (bf16[1,1,2048,384]{2,3,1,0:T(8,128)(2,1)S(1)}, bf16[1,1,2048,384]{2,3,1,0:T(8,128)(2,1)}, u32[]{:S(2)}) copy-start(bf16[1,1,2048,384]{2,3,1,0:T(8,128)(2,1)} %copy.13) | copy-start | bytes 4718596
  229.9 96.3 %collective-permute-start.4 = (bf16[1,1,2048,384]{3,2,1,0:T(8,128)(2,1)}, bf16[1,1,2048,384]{3,2,1,0:T(8,128)(2,1)}, u32[]{:S(2)}, u32[]{:S(2)}) collective-permute-start(bf16[1,1,2048,384]{3,2,1,0:T(8,128)(2,1)} %copy.20), channel_id=1, source_target_pairs={{0,32},{16,48},{32,64},{48,80},{64,96},{80,112},{96,128},{112,144}... | collective-permute-start | bytes 4718600 | tf_op jit(solution)/shard_map/cond/branch_1_fun/ppermute | solution.py:21
  232.9 96.4 %collective-permute-start.6 = (bf16[1,1,2048,384]{3,2,1,0:T(8,128)(2,1)}, bf16[1,1,2048,384]{3,2,1,0:T(8,128)(2,1)}, u32[]{:S(2)}, u32[]{:S(2)}) collective-permute-start(bf16[1,1,2048,384]{3,2,1,0:T(8,128)(2,1)} %copy.21), channel_id=1, source_target_pairs={{0,32},{16,48},{32,64},{48,80},{64,96},{80,112},{96,128},{112,144}... | collective-permute-start | bytes 4718600 | tf_op jit(solution)/shard_map/cond/branch_1_fun/ppermute | solution.py:21
  234.4 79.5 %collective-permute-start.5 = (bf16[1,1,128,2048]{3,2,1,0:T(8,128)(2,1)}, bf16[1,1,128,2048]{3,2,1,0:T(8,128)(2,1)S(1)}, u32[]{:S(2)}, u32[]{:S(2)}) collective-permute-start(bf16[1,1,128,2048]{3,2,1,0:T(8,128)(2,1)} %get-tuple-element.165), channel_id=1, source_target_pairs={{0,32},{16,48},{32,64},{48,80},{64,96},{80,112},{96,128},{112,144}... | collective-permute-start | bytes 1572872 | tf_op jit(solution)/shard_map/cond/branch_1_fun/ppermute | solution.py:21
  235.8 89.3 %collective-permute-start.7 = (bf16[1,1,128,2048]{3,2,1,0:T(8,128)(2,1)}, bf16[1,1,128,2048]{3,2,1,0:T(8,128)(2,1)S(1)}, u32[]{:S(2)}, u32[]{:S(2)}) collective-permute-start(bf16[1,1,128,2048]{3,2,1,0:T(8,128)(2,1)} %get-tuple-element.167), channel_id=1, source_target_pairs={{0,32},{16,48},{32,64},{48,80},{64,96},{80,112},{96,128},{112,144}... | collective-permute-start | bytes 1572872 | tf_op jit(solution)/shard_map/cond/branch_1_fun/ppermute | solution.py:21
  338.2 2.7 copy-start
  338.2 2.7 copy-start.2
Sparse Core Ops, SparseCore 0:
  11.3 168.4 all-gather.1
